TPU v7x, 32 devices: a whole 2x2x4 slice. The times are simulated.
32 devices in a mesh: batch: 4 (over y, x), ctx: 8 (over z, core).
Axes of the slice: x: 2, y: 2, z: 4, core: 2. Of those that a mesh axis runs over, the one named last changes fastest.
Arguments:
- inputs: float32 [4, 1024, 2304], P('batch', 'ctx'), may hold values from -6 to 6
- block_order: int32 [4, 8], P('batch'), may hold values from 0 to 7, each once within a row
- cotangent: float32 [4, 1024, 2304], P('batch', 'ctx'), may hold values from -6 to 6
- attn_gain: bfloat16 [2304], P(('batch', 'ctx')), may hold values from 0.5 to 1.5
- post_attn_gain: bfloat16 [2304], P(('batch', 'ctx')), may hold values from 0.5 to 1.5
- ffn_gain: bfloat16 [2304], P(('batch', 'ctx')), may hold values from 0.5 to 1.5
- post_ffn_gain: bfloat16 [2304], P(('batch', 'ctx')), may hold values from 0.5 to 1.5
- query_weight: bfloat16 [2304, 2048], P(('batch', 'ctx')), may hold values from -0.5 to 0.5
- key_weight: bfloat16 [2304, 1024], P(('batch', 'ctx')), may hold values from -0.125 to 0.125
- value_weight: bfloat16 [2304, 1024], P(('batch', 'ctx')), may hold values from -0.125 to 0.125
- out_weight: bfloat16 [2048, 2304], P(('batch', 'ctx')), may hold values from -0.125 to 0.125
- gate_weight: bfloat16 [9216, 2304], P(('batch', 'ctx')), may hold values from -0.125 to 0.125
- up_weight: bfloat16 [9216, 2304], P(('batch', 'ctx')), may hold values from -0.125 to 0.125
- down_weight: bfloat16 [9216, 2304], P(('batch', 'ctx')), may hold values from -0.0625 to 0.0625
Outputs:
- output: float32 [4, 1024, 2304], P('batch', 'ctx')
- input_grad: float32 [4, 1024, 2304], P('batch', 'ctx')
- query_grad: float32 [2304, 2048], P(('batch', 'ctx'))
- key_grad: float32 [2304, 1024], P(('batch', 'ctx'))
- value_grad: float32 [2304, 1024], P(('batch', 'ctx'))
- out_grad: float32 [2048, 2304], P(('batch', 'ctx'))
- gate_grad: float32 [9216, 2304], P(('batch', 'ctx'))
- up_grad: float32 [9216, 2304], P(('batch', 'ctx'))
- down_grad: float32 [9216, 2304], P(('batch', 'ctx'))
- attn_gain_grad: float32 [2304], P(('batch', 'ctx'))
- post_attn_gain_grad: float32 [2304], P(('batch', 'ctx'))
- ffn_gain_grad: float32 [2304], P(('batch', 'ctx'))
- post_ffn_gain_grad: float32 [2304], P(('batch', 'ctx'))
Inputs may be any that keep to these rules, and one draw needn't show every extreme that they name: Each row of block_order names every block of 128 positions of its sequence exactly once.
All inputs are finite; a program needn't handle non-finite values.
Results may differ from a plain program's by a relative error of at most 0.02.
The roundings to bfloat16 on the way count: a program that leaves them out, or rounds other values in their place, can miss the bound.
Values may be sent and summed in bfloat16 or wider, within the bound.
No kernel may reach another device: no remote copies, remote signals or barrier semaphores. Data moves between devices by JAX's collectives and lax.ppermute only.
A program may use at most 512 MiB of HBM per device.

v0:
```python
import math
import jax
import jax.numpy as jnp
from jax import lax
from jax.sharding import PartitionSpec as P

HEADS = 8
KV_HEADS = 4
HEAD_DIM = 256
NORM_EPS = 1e-06
SOFT_CAP = 50.0


def normalize(values_in, gain_vec):
    inv_rms = lax.rsqrt(jnp.mean(values_in * values_in, axis=-1, keepdims=True) + NORM_EPS)
    return (values_in * inv_rms * gain_vec.astype(jnp.float32), inv_rms)


def norm_back(values_in, inv_rms, gain_vec, grad_in):
    scaled = values_in * inv_rms
    weighted = grad_in * gain_vec.astype(jnp.float32)
    grad_gain = jnp.sum(grad_in * scaled, axis=0)
    grad_values = inv_rms * (
        weighted - scaled * jnp.mean(weighted * scaled, axis=-1, keepdims=True)
    )
    return (grad_values, grad_gain)


def geglu(gate_val, up_val):
    return jax.nn.gelu(gate_val, approximate=True) * up_val


def rows_product(left_mat, right_mat):
    return lax.dot_general(
        left_mat, right_mat, (((1,), (1,)), ((), ())), preferred_element_type=jnp.float32
    )


def cols_product(left_mat, right_mat):
    return lax.dot_general(
        left_mat, right_mat, (((0,), (0,)), ((), ())), preferred_element_type=jnp.float32
    )


def key_positions(block_row, row_count, local_rows):
    row_index = jnp.arange(row_count, dtype=jnp.int32)
    which_block = row_index // local_rows
    block_ids = jnp.arange(block_row.shape[0], dtype=jnp.int32)
    matches = which_block[:, None] == block_ids[None, :]
    chosen = jnp.sum(jnp.where(matches, block_row[None, :], 0), axis=1)
    return chosen * local_rows + row_index % local_rows


def on_device(
    inputs,
    block_order,
    cotangent,
    attn_gain,
    post_attn_gain,
    ffn_gain,
    post_ffn_gain,
    query_weight,
    key_weight,
    value_weight,
    out_weight,
    gate_weight,
    up_weight,
    down_weight,
):
    local_rows = inputs.shape[1]
    features = inputs.shape[2]
    rows_x = inputs.reshape(local_rows, features)
    grad_y = cotangent.reshape(local_rows, features)
    block_row = block_order.reshape(-1)
    block_count = block_row.shape[0]
    seq_length = local_rows * block_count
    groups = KV_HEADS
    ratio = HEADS // KV_HEADS
    key_width = KV_HEADS * HEAD_DIM
    scale = 1.0 / math.sqrt(HEAD_DIM)
    ctx_index = lax.axis_index("ctx")
    own_block = jnp.sum(
        jnp.where(jnp.arange(block_count, dtype=jnp.int32) == ctx_index, block_row, 0)
    )
    query_pos = own_block * local_rows + jnp.arange(local_rows, dtype=jnp.int32)
    gathered = (
        lax.all_gather(query_weight, ("batch", "ctx"), axis=0, tiled=True),
        lax.all_gather(key_weight, ("batch", "ctx"), axis=0, tiled=True),
        lax.all_gather(value_weight, ("batch", "ctx"), axis=0, tiled=True),
        lax.all_gather(out_weight, ("batch", "ctx"), axis=0, tiled=True),
        lax.all_gather(attn_gain, ("batch", "ctx"), axis=0, tiled=True),
        lax.all_gather(post_attn_gain, ("batch", "ctx"), axis=0, tiled=True),
        lax.all_gather(ffn_gain, ("batch", "ctx"), axis=0, tiled=True),
        lax.all_gather(post_ffn_gain, ("batch", "ctx"), axis=0, tiled=True),
    )
    w_query, w_key, w_value, w_out, gain_one, gain_two, gain_three, gain_four = gathered
    normed, inv_one = normalize(rows_x, gain_one)
    normed_in = normed.astype(jnp.bfloat16)
    query = jnp.dot(normed_in, w_query, preferred_element_type=jnp.float32).astype(jnp.bfloat16)
    kv_local = jnp.concatenate(
        (
            jnp.dot(normed_in, w_key, preferred_element_type=jnp.float32),
            jnp.dot(normed_in, w_value, preferred_element_type=jnp.float32),
        ),
        axis=1,
    ).astype(jnp.bfloat16)
    q_heads = query.reshape(local_rows, groups, ratio, HEAD_DIM)
    shard_piece = lax.all_gather(kv_local, "ctx", axis=0, tiled=True)
    row_count = shard_piece.shape[0]
    key_heads = shard_piece[:, :key_width].reshape(row_count, groups, HEAD_DIM)
    value_heads = shard_piece[:, key_width:].reshape(row_count, groups, HEAD_DIM)
    key_pos = key_positions(block_row, row_count, local_rows)
    visible = key_pos[None, :] <= query_pos[:, None]
    tanh_val = jnp.tanh(
        jnp.einsum("tgrd,jgd->grtj", q_heads, key_heads, preferred_element_type=jnp.float32)
        * scale
        / SOFT_CAP
    )
    raw = jnp.where(visible, jnp.exp(SOFT_CAP * tanh_val), 0.0)
    accum = jnp.einsum(
        "grtj,jgd->tgrd", raw.astype(jnp.bfloat16), value_heads, preferred_element_type=jnp.float32
    )
    totals = jnp.sum(raw, axis=3)
    accum, totals, kv_all = (accum, totals, shard_piece)
    attended = (
        (accum / jnp.transpose(totals, (2, 0, 1))[..., None])
        .reshape(local_rows, HEADS * HEAD_DIM)
        .astype(jnp.bfloat16)
    )
    branch = jnp.dot(attended, w_out, preferred_element_type=jnp.float32)
    branch_normed, inv_two = normalize(branch, gain_two)
    middle = rows_x + branch_normed
    normed_m, inv_three = normalize(middle, gain_three)
    normed_mid = normed_m.astype(jnp.bfloat16)
    gate_piece = lax.all_gather(gate_weight, ("batch", "ctx"), axis=0, tiled=True)
    up_piece = lax.all_gather(up_weight, ("batch", "ctx"), axis=0, tiled=True)
    down_piece = lax.all_gather(down_weight, ("batch", "ctx"), axis=0, tiled=True)
    hidden_piece = geglu(
        rows_product(normed_mid, gate_piece), rows_product(normed_mid, up_piece)
    ).astype(jnp.bfloat16)
    ffn_out = jnp.dot(hidden_piece, down_piece, preferred_element_type=jnp.float32)
    ffn_normed, inv_four = normalize(ffn_out, gain_four)
    output = middle + ffn_normed
    grad_ffn, grad_four = norm_back(ffn_out, inv_four, gain_four, grad_y)
    grad_ffn_b = grad_ffn.astype(jnp.bfloat16)
    gate_piece = lax.all_gather(gate_weight, ("batch", "ctx"), axis=0, tiled=True)
    up_piece = lax.all_gather(up_weight, ("batch", "ctx"), axis=0, tiled=True)
    down_piece = lax.all_gather(down_weight, ("batch", "ctx"), axis=0, tiled=True)
    gate_act = rows_product(normed_mid, gate_piece)
    up_act = rows_product(normed_mid, up_piece)
    hidden_f, pull_back = jax.vjp(geglu, gate_act, up_act)
    grad_gate, grad_up = pull_back(rows_product(grad_ffn_b, down_piece))
    grad_gate_b = grad_gate.astype(jnp.bfloat16)
    grad_up_b = grad_up.astype(jnp.bfloat16)
    grad_nm = jnp.dot(grad_gate_b, gate_piece, preferred_element_type=jnp.float32) + jnp.dot(
        grad_up_b, up_piece, preferred_element_type=jnp.float32
    )
    rows_piece = lax.all_gather(normed_mid, ("batch", "ctx"), axis=0, tiled=True)
    cot_piece = lax.all_gather(grad_ffn_b, ("batch", "ctx"), axis=0, tiled=True)
    gate_act = rows_product(rows_piece, gate_weight)
    up_act = rows_product(rows_piece, up_weight)
    hidden_f, pull_back = jax.vjp(geglu, gate_act, up_act)
    grad_gate, grad_up = pull_back(rows_product(cot_piece, down_weight))
    gate_acc = cols_product(grad_gate.astype(jnp.bfloat16), rows_piece)
    up_acc = cols_product(grad_up.astype(jnp.bfloat16), rows_piece)
    down_acc = cols_product(hidden_f.astype(jnp.bfloat16), cot_piece)
    grad_mid_part, grad_three = norm_back(middle, inv_three, gain_three, grad_nm)
    grad_mid = grad_y + grad_mid_part
    grad_branch, grad_two = norm_back(branch, inv_two, gain_two, grad_mid)
    grad_branch_b = grad_branch.astype(jnp.bfloat16)
    out_term = cols_product(attended, grad_branch_b)
    grad_att = rows_product(grad_branch_b, w_out).astype(jnp.bfloat16)
    ga_heads = grad_att.reshape(local_rows, groups, ratio, HEAD_DIM)
    at_heads = attended.reshape(local_rows, groups, ratio, HEAD_DIM)
    delta = jnp.transpose(
        jnp.sum(ga_heads.astype(jnp.float32) * at_heads.astype(jnp.float32), axis=3), (1, 2, 0)
    )
    key_all = kv_all[:, :key_width].reshape(seq_length, groups, HEAD_DIM)
    value_all = kv_all[:, key_width:].reshape(seq_length, groups, HEAD_DIM)
    key_pos = key_positions(block_row, seq_length, local_rows)
    visible = key_pos[None, :] <= query_pos[:, None]
    tanh_val = jnp.tanh(
        jnp.einsum("tgrd,jgd->grtj", q_heads, key_all, preferred_element_type=jnp.float32)
        * scale
        / SOFT_CAP
    )
    prob = jnp.where(visible, jnp.exp(SOFT_CAP * tanh_val) / totals[..., None], 0.0)
    dprob = jnp.einsum("tgrd,jgd->grtj", ga_heads, value_all, preferred_element_type=jnp.float32)
    grad_z = (prob * (dprob - delta[..., None]) * (1.0 - tanh_val * tanh_val) * scale).astype(
        jnp.bfloat16
    )
    grad_query = (
        jnp.einsum("grtj,jgd->tgrd", grad_z, key_all, preferred_element_type=jnp.float32)
        .reshape(local_rows, HEADS * HEAD_DIM)
        .astype(jnp.bfloat16)
    )
    key_terms = jnp.einsum(
        "grtj,tgrd->jgd", grad_z, q_heads, preferred_element_type=jnp.float32
    ).reshape(seq_length, key_width)
    value_terms = jnp.einsum(
        "grtj,tgrd->jgd", prob.astype(jnp.bfloat16), ga_heads, preferred_element_type=jnp.float32
    ).reshape(seq_length, key_width)
    kv_terms = jnp.concatenate((key_terms, value_terms), axis=1)
    kv_own = lax.psum_scatter(kv_terms.astype(jnp.bfloat16), "ctx", scatter_dimension=0, tiled=True)
    grad_keys = kv_own[:, :key_width]
    grad_values = kv_own[:, key_width:]
    query_term = cols_product(normed_in, grad_query)
    key_term = cols_product(normed_in, grad_keys)
    value_term = cols_product(normed_in, grad_values)
    grad_in = (
        rows_product(grad_query, w_query)
        + rows_product(grad_keys, w_key)
        + rows_product(grad_values, w_value)
    )
    grad_x_part, grad_one = norm_back(rows_x, inv_one, gain_one, grad_in)
    input_grad = grad_mid + grad_x_part
    summed = (
        lax.psum_scatter(query_term, ("batch", "ctx"), scatter_dimension=0, tiled=True),
        lax.psum_scatter(key_term, ("batch", "ctx"), scatter_dimension=0, tiled=True),
        lax.psum_scatter(value_term, ("batch", "ctx"), scatter_dimension=0, tiled=True),
        lax.psum_scatter(out_term, ("batch", "ctx"), scatter_dimension=0, tiled=True),
        lax.psum_scatter(grad_one, ("batch", "ctx"), scatter_dimension=0, tiled=True),
        lax.psum_scatter(grad_two, ("batch", "ctx"), scatter_dimension=0, tiled=True),
        lax.psum_scatter(grad_three, ("batch", "ctx"), scatter_dimension=0, tiled=True),
        lax.psum_scatter(grad_four, ("batch", "ctx"), scatter_dimension=0, tiled=True),
    )
    (
        query_grad,
        key_grad,
        value_grad,
        out_grad,
        attn_gain_grad,
        post_attn_gain_grad,
        ffn_gain_grad,
        post_ffn_gain_grad,
    ) = summed
    return (
        output.reshape(1, local_rows, features),
        input_grad.reshape(1, local_rows, features),
        query_grad,
        key_grad,
        value_grad,
        out_grad,
        gate_acc,
        up_acc,
        down_acc,
        attn_gain_grad,
        post_attn_gain_grad,
        ffn_gain_grad,
        post_ffn_gain_grad,
    )


def solution(mesh):
    return jax.shard_map(
        on_device,
        mesh=mesh,
        in_specs=(
            P("batch", "ctx", None),
            P("batch", None),
            P("batch", "ctx", None),
            P(("batch", "ctx")),
            P(("batch", "ctx")),
            P(("batch", "ctx")),
            P(("batch", "ctx")),
            P(("batch", "ctx"), None),
            P(("batch", "ctx"), None),
            P(("batch", "ctx"), None),
            P(("batch", "ctx"), None),
            P(("batch", "ctx"), None),
            P(("batch", "ctx"), None),
            P(("batch", "ctx"), None),
        ),
        out_specs=(
            P("batch", "ctx", None),
            P("batch", "ctx", None),
            P(("batch", "ctx"), None),
            P(("batch", "ctx"), None),
            P(("batch", "ctx"), None),
            P(("batch", "ctx"), None),
            P(("batch", "ctx"), None),
            P(("batch", "ctx"), None),
            P(("batch", "ctx"), None),
            P(("batch", "ctx")),
            P(("batch", "ctx")),
            P(("batch", "ctx")),
            P(("batch", "ctx")),
        ),
        check_vma=False,
    )
```

profile of v0, /device:TPU:0, one launch (start us, length us, event | category | flops | bytes accessed | tf_op | source)
XLA Modules:
  0.0 2215.7 jit_solution(690600870943740185)
XLA Ops:
  12.1 42.5 %all-reduce.9 = (bf16[2304]{0:T(1024)(128)(2,1)S(1)}, bf16[2304]{0:T(1024)(128)(2,1)S(1)}, bf16[2304]{0:T(1024)(128)(2,1)S(1)}, bf16[2304]{0:T(1024)(128)(2,1)S(1)}) all-reduce(bf16[2304]{0:T(1024)(128)(2,1)S(1)} %dynamic-update-slice, bf16[2304]{0:T(1024)(128)(2,1)S(1)} %dynamic-update-slice.1, ...), channel_id=1, replica_groups=mesh['batch'=4,'ctx'=8] {'batch','ctx'}, use_global_device_ids=true, to_apply=%add | all-reduce | flops 9216 | bytes 36864
  58.2 19.2 all-gather.13.cloned.1.call-done
  80.5 61.8 %all-gather.11.cloned.1.call-done = bf16[2304,1024]{1,0:T(8,128)(2,1)} async-done(((bf16[72,1024]{1,0:T(8,128)(2,1)}), bf16[2304,1024]{1,0:T(8,128)(2,1)}) %all-gather.11.cloned.1.call-update) | async-done | bytes 4718608 | tf_op jit(solution)/shard_map/all_gather | solution.py:88
  152.1 39.6 %all-gather.15.cloned.1.call-done = bf16[1024,2048]{1,0:T(8,128)(2,1)} async-done(((bf16[128,2048]{1,0:T(8,128)(2,1)}), bf16[1024,2048]{1,0:T(8,128)(2,1)}) %all-gather.15.cloned.1.call-update) | async-done | bytes 4194320 | tf_op jit(solution)/shard_map/all_gather | solution.py:108
  209.6 65.3 %all-gather.17.cloned.1.call-done = bf16[2304,2048]{1,0:T(8,128)(2,1)} async-done(((bf16[72,2048]{1,0:T(8,128)(2,1)}), bf16[2304,2048]{1,0:T(8,128)(2,1)}) %all-gather.17.cloned.1.call-update) | async-done | bytes 9437200 | tf_op jit(solution)/shard_map/all_gather | solution.py:87
  287.3 70.6 %all-gather.19.cloned.1.call-done = bf16[2048,2304]{1,0:T(8,128)(2,1)} async-done(((bf16[64,2304]{1,0:T(8,128)(2,1)}), bf16[2048,2304]{1,0:T(8,128)(2,1)}) %all-gather.19.cloned.1.call-update) | async-done | bytes 9437200 | tf_op jit(solution)/shard_map/all_gather | solution.py:90
  365.3 231.1 %all-gather.23.cloned.1.call-done = bf16[9216,2304]{1,0:T(8,128)(2,1)} async-done(((bf16[288,2304]{1,0:T(8,128)(2,1)}), bf16[9216,2304]{1,0:T(8,128)(2,1)}) %all-gather.23.cloned.1.call-update) | async-done | bytes 42467344 | tf_op jit(solution)/shard_map/all_gather | solution.py:136
  596.4 22.3 %fusion.117 = f32[128,9216]{1,0:T(8,128)} fusion(bf16[128,2304]{1,0:T(8,128)(2,1)S(1)} %multiply_convert_fusion.11, bf16[9216,2304]{1,0:T(8,128)(2,1)} %all-gather.23.cloned.1.call-done), kind=kOutput, calls=%fused_computation.174 | convolution fusion | flops 5435817984 | bytes 47775744 | tf_op jit(solution)/shard_map/dot_general | solution.py:34
  618.7 215.9 %all-gather.21.cloned.1.call-done = bf16[9216,2304]{1,0:T(8,128)(2,1)} async-done(((bf16[288,2304]{1,0:T(8,128)(2,1)}), bf16[9216,2304]{1,0:T(8,128)(2,1)}) %all-gather.21.cloned.1.call-update) | async-done | bytes 42467344 | tf_op jit(solution)/shard_map/all_gather | solution.py:135
  834.6 22.4 %fusion.116 = f32[128,9216]{1,0:T(8,128)} fusion(bf16[128,2304]{1,0:T(8,128)(2,1)S(1)} %multiply_convert_fusion.11, bf16[9216,2304]{1,0:T(8,128)(2,1)} %all-gather.21.cloned.1.call-done), kind=kOutput, calls=%fused_computation.173 | convolution fusion | flops 5435817984 | bytes 47775744 | tf_op jit(solution)/shard_map/dot_general | solution.py:34
  857.0 215.8 %all-gather.25.cloned.1.call-done = bf16[9216,2304]{1,0:T(8,128)(2,1)} async-done(((bf16[288,2304]{1,0:T(8,128)(2,1)}), bf16[9216,2304]{1,0:T(8,128)(2,1)}) %all-gather.25.cloned.1.call-update) | async-done | bytes 42467344 | tf_op jit(solution)/shard_map/all_gather | solution.py:137
  1072.9 20.8 multiply_reduce_fusion.7
  1099.2 21.7 fusion.118
  1120.9 21.8 fusion.25
  1142.7 25.3 %multiply_reduce_fusion = (f32[2304]{0:T(1024)}, f32[128]{0:T(128)S(1)}, f32[128,2304]{1,0:T(8,128)}) fusion(f32[128,2304]{1,0:T(8,128)S(1)} %get-tuple-element.31, f32[128]{0:T(128)} %copy-done.27, f32[2304]{0:T(1024)S(1)} %convert_element_type.99, f32[128,2304]{1,0:T(8,128)} %fusion.25, bf16[9216,2304]{1,0:T(8,128)(2,1)} %all-gather.23.cloned.1.call-done, ...), kind=kOutput, calls=%fused_computation.82 | convolution fusion | flops 5449676800 | bytes 55462912 | tf_op jit(solution)/shard_map/dot_general | solution.py:155
  1172.6 6.9 convolution_convert_fusion
  1201.3 46.9 %reduce-scatter.16.cloned.1.call-done = bf16[128,2048]{1,0:T(8,128)(2,1)} async-done(((bf16[1024,2048]{1,0:T(8,128)(2,1)}), bf16[128,2048]{1,0:T(8,128)(2,1)}) %reduce-scatter.16.cloned.1.call-update) | async-done | bytes 524304
  1263.4 8.2 fusion.62
  1271.7 8.0 fusion.120
  1279.7 93.9 %all-gather.29.cloned.1.call-done = bf16[4096,2304]{1,0:T(8,128)(2,1)} async-done(((bf16[128,2304]{1,0:T(8,128)(2,1)}), bf16[4096,2304]{1,0:T(8,128)(2,1)}) %all-gather.29.cloned.1.call-update) | async-done | bytes 18874384 | tf_op jit(solution)/shard_map/all_gather | solution.py:158
  1373.5 11.5 fusion.123
  1385.0 12.8 fusion.122
  1405.2 42.1 %all-reduce.8 = (f32[2304]{0:T(1024)}, f32[2304]{0:T(1024)}, f32[2304]{0:T(1024)}, f32[2304]{0:T(1024)}) all-reduce(f32[2304]{0:T(1024)} %get-tuple-element.19, f32[2304]{0:T(1024)} %get-tuple-element.17, f32[2304]{0:T(1024)} %get-tuple-element.15, f32[2304]{0:T(1024)} %get-tuple-element.13), channel_id=7, replica_groups=mesh['batch'=4,'ctx'=8] {'batch','ctx'}, use_global_device_ids=true, to_apply=%region_18.19.clone | all-reduce | flops 9216 | bytes 73728
  1454.4 46.2 %all-gather.27.cloned.1.call-done = bf16[4096,2304]{1,0:T(8,128)(2,1)} async-done(((bf16[128,2304]{1,0:T(8,128)(2,1)}), bf16[4096,2304]{1,0:T(8,128)(2,1)}) %all-gather.27.cloned.1.call-update) | async-done | bytes 18874384 | tf_op jit(solution)/shard_map/all_gather | solution.py:159
  1500.6 13.3 fusion.121
  1513.9 16.9 fusion.21
  1530.8 11.3 fusion.22
  1542.1 21.0 fusion.23
  1563.1 78.3 %reduce-scatter.10.cloned.1.call-done = f32[72,1024]{1,0:T(8,128)} async-done(((f32[2304,1024]{1,0:T(8,128)}), f32[72,1024]{1,0:T(8,128)}) %reduce-scatter.10.cloned.1.call-update) | async-done | bytes 294928 | tf_op jit(solution)/shard_map/reduce_scatter | solution.py:219
  1641.4 141.7 %reduce-scatter.12.cloned.1.call-done = f32[72,1024]{1,0:T(8,128)} async-done(((f32[2304,1024]{1,0:T(8,128)}), f32[72,1024]{1,0:T(8,128)}) %reduce-scatter.12.cloned.1.call-update) | async-done | bytes 294928 | tf_op jit(solution)/shard_map/reduce_scatter | solution.py:220
  1783.0 212.6 %reduce-scatter.8.cloned.1.call-done = f32[72,2048]{1,0:T(8,128)} async-done(((f32[2304,2048]{1,0:T(8,128)}), f32[72,2048]{1,0:T(8,128)}) %reduce-scatter.8.cloned.1.call-update) | async-done | bytes 589840 | tf_op jit(solution)/shard_map/reduce_scatter | solution.py:218
  1995.7 213.0 %reduce-scatter.14.cloned.1.call-done = f32[64,2304]{1,0:T(8,128)} async-done(((f32[2048,2304]{1,0:T(8,128)}), f32[64,2304]{1,0:T(8,128)}) %reduce-scatter.14.cloned.1.call-update) | async-done | bytes 589840 | tf_op jit(solution)/shard_map/reduce_scatter | solution.py:221
  (190 shorter events, 119.5 us)
Async XLA Ops:
  7.2 70.2 %all-gather.13.cloned.1.call-start = ((), (), s32[]{:S(2)}) async-start(), calls=%async_computation.6 | async-start | bytes 4866048 | tf_op jit(solution)/shard_map/all_gather | solution.py:89
  7.9 134.4 %all-gather.11.cloned.1.call-start = ((), (), s32[]{:S(2)}) async-start(), calls=%async_computation.5 | async-start | bytes 4866048 | tf_op jit(solution)/shard_map/all_gather | solution.py:88
  8.7 183.0 %all-gather.15.cloned.1.call-start = ((), (), s32[]{:S(2)}) async-start(), calls=%async_computation.7 | async-start | bytes 4718592 | tf_op jit(solution)/shard_map/all_gather | solution.py:108
  146.4 128.6 %all-gather.17.cloned.1.call-start = ((), (), s32[]{:S(2)}) async-start(), calls=%async_computation.8 | async-start | bytes 9732096 | tf_op jit(solution)/shard_map/all_gather | solution.py:87
  146.9 211.0 %all-gather.19.cloned.1.call-start = ((), (), s32[]{:S(2)}) async-start(), calls=%async_computation.9 | async-start | bytes 9732096 | tf_op jit(solution)/shard_map/all_gather | solution.py:90
  147.5 448.9 %all-gather.23.cloned.1.call-start = ((), (), s32[]{:S(2)}) async-start(), calls=%async_computation.11 | async-start | bytes 43794432 | tf_op jit(solution)/shard_map/all_gather | solution.py:136
  148.1 686.5 %all-gather.21.cloned.1.call-start = ((), (), s32[]{:S(2)}) async-start(), calls=%async_computation.10 | async-start | bytes 43794432 | tf_op jit(solution)/shard_map/all_gather | solution.py:135
  148.8 924.0 %all-gather.25.cloned.1.call-start = ((), (), s32[]{:S(2)}) async-start(), calls=%async_computation.12 | async-start | bytes 43794432 | tf_op jit(solution)/shard_map/all_gather | solution.py:137
  149.6 1098.6 %reduce-scatter.16.cloned.1.call-start = ((), (), s32[]{:S(2)}) async-start(), calls=%async_computation.19 | async-start | bytes 4718592
  149.9 213.4 %copy-start.20 = (f32[2304]{0:T(1024)}, f32[2304]{0:T(1024)S(1)}, u32[]{:S(2)}) copy-start(f32[2304]{0:T(1024)S(1)} %convert_element_type.98) | copy-start | bytes 27652
  152.1 131.7 %copy-start.22 = (pred[128,1024]{0,1:T(8,128)(4,1)}, pred[128,1024]{0,1:T(8,128)(4,1)S(1)}, u32[]{:S(2)}) copy-start(pred[128,1024]{0,1:T(8,128)(4,1)S(1)} %broadcast_compare_fusion) | copy-start | bytes 393220
  287.3 75.9 %copy-start.6 = (bf16[128,4,2,256]{0,3,2,1:T(8,128)(2,1)}, bf16[128,4,2,256]{0,3,2,1:T(8,128)(2,1)S(1)}, u32[]{:S(2)}) copy-start(bf16[128,4,2,256]{0,3,2,1:T(8,128)(2,1)S(1)} %divide_convert_fusion) | copy-start | bytes 1572868
  365.3 469.3 %copy-start.5 = (bf16[128,2304]{1,0:T(8,128)(2,1)}, bf16[128,2304]{1,0:T(8,128)(2,1)S(1)}, u32[]{:S(2)}) copy-start(bf16[128,2304]{1,0:T(8,128)(2,1)S(1)} %multiply_convert_fusion.11) | copy-start | bytes 1769476
  857.0 236.6 %copy-start.24 = (f32[2304]{0:T(1024)S(1)}, f32[2304]{0:T(1024)}, u32[]{:S(2)}) copy-start(f32[2304]{0:T(1024)} %convert_element_type.102) | copy-start | bytes 27652
  1099.2 21.7 copy-start.8
  1142.7 25.3 %copy-start.21 = (f32[2304]{0:T(1024)S(1)}, f32[2304]{0:T(1024)}, u32[]{:S(2)}) copy-start(f32[2304]{0:T(1024)} %copy-done.20) | copy-start | bytes 27652
  1142.7 25.3 %copy-start.28 = (f32[128]{0:T(128)S(1)}, f32[128]{0:T(128)}, u32[]{:S(2)}) copy-start(f32[128]{0:T(128)} %copy-done.27) | copy-start | bytes 1540
  1199.9 173.6 %all-gather.29.cloned.1.call-start = ((), (), s32[]{:S(2)}) async-start(), calls=%async_computation.18 | async-start | bytes 19464192 | tf_op jit(solution)/shard_map/all_gather | solution.py:158
  1200.5 300.1 %all-gather.27.cloned.1.call-start = ((), (), s32[]{:S(2)}) async-start(), calls=%async_computation.17 | async-start | bytes 19464192 | tf_op jit(solution)/shard_map/all_gather | solution.py:159
  1201.2 440.2 %reduce-scatter.10.cloned.1.call-start = ((), (), s32[]{:S(2)}) async-start(), calls=%async_computation.14 | async-start | bytes 9732096 | tf_op jit(solution)/shard_map/reduce_scatter | solution.py:219
  1254.2 528.8 %reduce-scatter.12.cloned.1.call-start = ((), (), s32[]{:S(2)}) async-start(), calls=%async_computation.15 | async-start | bytes 9732096 | tf_op jit(solution)/shard_map/reduce_scatter | solution.py:220
  1260.4 735.3 %reduce-scatter.8.cloned.1.call-start = ((), (), s32[]{:S(2)}) async-start(), calls=%async_computation.13 | async-start | bytes 19464192 | tf_op jit(solution)/shard_map/reduce_scatter | solution.py:218
  1271.6 937.0 %reduce-scatter.14.cloned.1.call-start = ((), (), s32[]{:S(2)}) async-start(), calls=%async_computation.16 | async-start | bytes 19464192 | tf_op jit(solution)/shard_map/reduce_scatter | solution.py:221
  1373.5 24.3 %slice-start = ((s8[9437184]{0:T(1024)(128)(4,1)}), s8[4194304]{0:T(1024)(128)(4,1)S(1)}, s32[]{:S(2)}) async-start(s8[9437184]{0:T(1024)(128)(4,1)} %bitcast.141), calls=%async_computation.20 | async-start | bytes 8388608
  1373.5 24.3 %slice-start.1 = ((s8[9437184]{0:T(1024)(128)(4,1)}), s8[4194304]{0:T(1024)(128)(4,1)S(1)}, s32[]{:S(2)}) async-start(s8[9437184]{0:T(1024)(128)(4,1)} %bitcast.141), calls=%async_computation.21 | async-start | bytes 8388608
  1373.5 27.5 %slice-start.3 = ((s8[4718592]{0:T(1024)(128)(4,1)}), s8[4194304]{0:T(1024)(128)(4,1)S(1)}, s32[]{:S(2)}) async-start(s8[4718592]{0:T(1024)(128)(4,1)} %bitcast.143), calls=%async_computation.23 | async-start | bytes 8388608
  1373.5 29.2 %slice-start.5 = ((s8[4718592]{0:T(1024)(128)(4,1)}), s8[4194304]{0:T(1024)(128)(4,1)S(1)}, s32[]{:S(2)}) async-start(s8[4718592]{0:T(1024)(128)(4,1)} %bitcast.145), calls=%async_computation.25 | async-start | bytes 8388608
  1385.0 17.8 slice-start.6
  1402.8 50.3 %copy-start.4 = (f32[128,2304]{1,0:T(8,128)S(1)}, f32[128,2304]{1,0:T(8,128)}, u32[]{:S(2)}) copy-start(f32[128,2304]{1,0:T(8,128)} %copy-done.3) | copy-start | bytes 3538948
  1500.6 30.2 %slice-start.7 = ((s8[18874368]{0:T(1024)(128)(4,1)}), s8[4194304]{0:T(1024)(128)(4,1)S(1)}, s32[]{:S(2)}) async-start(s8[18874368]{0:T(1024)(128)(4,1)} %bitcast.162), calls=%async_computation.27 | async-start | bytes 8388608
  1500.6 30.2 %slice-start.8 = ((s8[18874368]{0:T(1024)(128)(4,1)}), s8[4194304]{0:T(1024)(128)(4,1)S(1)}, s32[]{:S(2)}) async-start(s8[18874368]{0:T(1024)(128)(4,1)} %bitcast.162), calls=%async_computation.28 | async-start | bytes 8388608
  1500.6 30.2 %slice-start.9 = ((s8[18874368]{0:T(1024)(128)(4,1)}), s8[4194304]{0:T(1024)(128)(4,1)S(1)}, s32[]{:S(2)}) async-start(s8[18874368]{0:T(1024)(128)(4,1)} %bitcast.162), calls=%async_computation.29 | async-start | bytes 8388608
  (29 other events, 161.4 us)
Sparse Core Ops, SparseCore 0:
  11.0 66.3 all-gather.12
  80.4 61.9 all-gather.10
  146.5 45.1 all-gather.14
  194.6 80.3 all-gather.16
  277.8 80.0 all-gather.18
  360.8 235.5 all-gather.22
  599.4 235.1 all-gather.20
  837.6 235.1 all-gather.24
  1200.0 48.0 reduce-scatter.15
  1251.0 122.4 all-gather.28
  1376.6 123.9 all-gather.26
  1506.9 134.4 reduce-scatter.9
  1647.9 135.1 reduce-scatter.11
  1789.9 205.7 reduce-scatter.7
  2002.5 206.0 reduce-scatter.13
where the time goes:
time: 2220 us
  waiting for transfers between devices  1760 us (79%)
  matrix products  294 us (13%)
  blocking collectives  84.6 us (4%)
  local copies, waits for them, and re-layouts  42 us (2%)
    all_gather x1, waiting for transfers between devices, on_device(): up_piece = lax.all_gather(up_weight, ('batch', 'ctx'), axis=0, tiled=True)  231 us
    all_gather x1, waiting for transfers between devices, on_device(): lax.all_gather(gate_weight, ('batch', 'ctx'), axis=0, tiled=True)  216 us
    all_gather x1, waiting for transfers between devices, on_device(): lax.all_gather(down_weight, ('batch', 'ctx'), axis=0, tiled=True)  216 us
    reduce_scatter x1, waiting for transfers between devices, on_device(): lax.psum_scatter(out_term, ('batch', 'ctx'), scatter_dimension=0, tiled=T...  213 us
    reduce_scatter x1, waiting for transfers between devices, on_device(): lax.psum_scatter(query_term, ('batch', 'ctx'), scatter_dimension=0, tiled...  213 us
    reduce_scatter x1, waiting for transfers between devices, on_device(): lax.psum_scatter(value_term, ('batch', 'ctx'), scatter_dimension=0, tiled...  142 us
    dot_general x10, matrix products, rows_product(): lax.dot_general(left_mat, right_mat, (((1,), (1,)), ((), ())), preferred_...  118 us
    all_gather x1, waiting for transfers between devices, on_device(): lax.all_gather(normed_mid, ('batch', 'ctx'), axis=0, tiled=True)  93.9 us
  transfers between devices with their start and end apart: 15, of which 15 were waited for; matrix products, arithmetic and copies ran while one was open for 10% of the time, Pallas kernels for 0%

commit v1 on v0

--- a/solution.py
+++ b/solution.py
@@ -9,6 +9,13 @@
 HEAD_DIM = 256
 NORM_EPS = 1e-06
 SOFT_CAP = 50.0
+
+
+def name_matrix(z_in, shard_in):
+    vec_out = jnp.concatenate([shard_in, z_in], 1)
+    part_next = lax.all_gather(vec_out, ("batch", "ctx"), axis=0, tiled=True)
+    all_rows = jnp.split(part_next, [shard_in.shape[1]], 1)
+    return all_rows
 
 
 def normalize(values_in, gain_vec):
@@ -133,8 +140,7 @@
     normed_m, inv_three = normalize(middle, gain_three)
     normed_mid = normed_m.astype(jnp.bfloat16)
     gate_piece = lax.all_gather(gate_weight, ("batch", "ctx"), axis=0, tiled=True)
-    up_piece = lax.all_gather(up_weight, ("batch", "ctx"), axis=0, tiled=True)
-    down_piece = lax.all_gather(down_weight, ("batch", "ctx"), axis=0, tiled=True)
+    up_piece, down_piece = name_matrix(down_weight, up_weight)
     hidden_piece = geglu(
         rows_product(normed_mid, gate_piece), rows_product(normed_mid, up_piece)
     ).astype(jnp.bfloat16)

time: 2220 us -> 2620 us (1.18)
  waiting for transfers between devices: 1760 us -> 2160 us
    all_gather x0 -> x1, waiting for transfers between devices: none -> 419 us  [name_matrix(): part_next = lax.all_gather(vec_out, ('batch', 'ctx'), axis=0, tiled=True)]
    dot_general x10 -> x9, matrix products: 118 us -> 97.6 us  [rows_product(): lax.dot_general(left_mat, right_mat, (((1,), (1,)), ((), ())), preferred_...]
    unnamed x16 -> x17, waiting for transfers between devices: 52.6 us -> 52.4 us
  transfers between devices with their start and end apart: 15 -> 16, of which waited for: 15 -> 16; matrix products, arithmetic and copies ran while one was open for 10% -> 10% of each run, Pallas kernels for 0% -> 0%
where the time goes in v1:
time: 2620 us
  waiting for transfers between devices  2160 us (82%)
  matrix products  294 us (11%)
  blocking collectives  84.7 us (3%)
  local copies, waits for them, and re-layouts  37.3 us (1%)
    all_gather x1, waiting for transfers between devices, name_matrix(): part_next = lax.all_gather(vec_out, ('batch', 'ctx'), axis=0, tiled=True)  419 us
    all_gather x1, waiting for transfers between devices, on_device(): lax.all_gather(gate_weight, ('batch', 'ctx'), axis=0, tiled=True)  233 us
    all_gather x1, waiting for transfers between devices, on_device(): up_piece = lax.all_gather(up_weight, ('batch', 'ctx'), axis=0, tiled=True)  216 us
    reduce_scatter x1, waiting for transfers between devices, on_device(): lax.psum_scatter(out_term, ('batch', 'ctx'), scatter_dimension=0, tiled=T...  213 us
    reduce_scatter x1, waiting for transfers between devices, on_device(): lax.psum_scatter(query_term, ('batch', 'ctx'), scatter_dimension=0, tiled...  213 us
    all_gather x1, waiting for transfers between devices, on_device(): lax.all_gather(down_weight, ('batch', 'ctx'), axis=0, tiled=True)  198 us
    reduce_scatter x1, waiting for transfers between devices, on_device(): lax.psum_scatter(value_term, ('batch', 'ctx'), scatter_dimension=0, tiled...  142 us
    dot_general x9, matrix products, rows_product(): lax.dot_general(left_mat, right_mat, (((1,), (1,)), ((), ())), preferred_...  97.6 us
  transfers between devices with their start and end apart: 16, of which 16 were waited for; matrix products, arithmetic and copies ran while one was open for 10% of the time, Pallas kernels for 0%

profile of v1, /device:TPU:0, one launch (start us, length us, event | category | flops | bytes accessed | tf_op | source)
XLA Modules:
  0.0 2617.5 jit_solution(2307980554319169842)
XLA Ops:
  12.1 42.5 %all-reduce.9 = (bf16[2304]{0:T(1024)(128)(2,1)S(1)}, bf16[2304]{0:T(1024)(128)(2,1)S(1)}, bf16[2304]{0:T(1024)(128)(2,1)S(1)}, bf16[2304]{0:T(1024)(128)(2,1)S(1)}) all-reduce(bf16[2304]{0:T(1024)(128)(2,1)S(1)} %dynamic-update-slice, bf16[2304]{0:T(1024)(128)(2,1)S(1)} %dynamic-update-slice.1, ...), channel_id=1, replica_groups=mesh['batch'=4,'ctx'=8] {'batch','ctx'}, use_global_device_ids=true, to_apply=%add | all-reduce | flops 9216 | bytes 36864
  58.2 19.2 all-gather.14.cloned.1.call-done
  80.5 61.8 %all-gather.12.cloned.1.call-done = bf16[2304,1024]{1,0:T(8,128)(2,1)} async-done(((bf16[72,1024]{1,0:T(8,128)(2,1)}), bf16[2304,1024]{1,0:T(8,128)(2,1)}) %all-gather.12.cloned.1.call-update) | async-done | bytes 4718608 | tf_op jit(solution)/shard_map/all_gather | solution.py:95
  153.8 37.8 %all-gather.16.cloned.1.call-done = bf16[1024,2048]{1,0:T(8,128)(2,1)} async-done(((bf16[128,2048]{1,0:T(8,128)(2,1)}), bf16[1024,2048]{1,0:T(8,128)(2,1)}) %all-gather.16.cloned.1.call-update) | async-done | bytes 4194320 | tf_op jit(solution)/shard_map/all_gather | solution.py:115
  207.2 67.8 %all-gather.18.cloned.1.call-done = bf16[2304,2048]{1,0:T(8,128)(2,1)} async-done(((bf16[72,2048]{1,0:T(8,128)(2,1)}), bf16[2304,2048]{1,0:T(8,128)(2,1)}) %all-gather.18.cloned.1.call-update) | async-done | bytes 9437200 | tf_op jit(solution)/shard_map/all_gather | solution.py:94
  285.6 72.3 %all-gather.20.cloned.1.call-done = bf16[2048,2304]{1,0:T(8,128)(2,1)} async-done(((bf16[64,2304]{1,0:T(8,128)(2,1)}), bf16[2048,2304]{1,0:T(8,128)(2,1)}) %all-gather.20.cloned.1.call-update) | async-done | bytes 9437200 | tf_op jit(solution)/shard_map/all_gather | solution.py:97
  363.8 232.5 %all-gather.22.cloned.1.call-done = bf16[9216,2304]{1,0:T(8,128)(2,1)} async-done(((bf16[288,2304]{1,0:T(8,128)(2,1)}), bf16[9216,2304]{1,0:T(8,128)(2,1)}) %all-gather.22.cloned.1.call-update) | async-done | bytes 42467344 | tf_op jit(solution)/shard_map/all_gather | solution.py:142
  596.4 23.7 fusion.123
  620.1 419.2 %all-gather.24.cloned.1.call-done = bf16[9216,4608]{1,0:T(8,128)(2,1)} async-done(((bf16[288,4608]{1,0:T(8,128)(2,1)}), bf16[9216,4608]{1,0:T(8,128)(2,1)}) %all-gather.24.cloned.1.call-update) | async-done | bytes 84934672 | tf_op jit(solution)/shard_map/all_gather | solution.py:16
  1039.3 34.0 %multiply_reduce_fusion.7 = (f32[128]{0:T(128)}, f32[128,2304]{1,0:T(8,128)}) fusion(bf16[9216,4608]{1,0:T(8,128)(2,1)} %all-gather.24.cloned.1.call-done, bf16[128,2304]{1,0:T(8,128)(2,1)} %copy-done.9, f32[128,9216]{1,0:T(8,128)} %fusion.123), kind=kOutput, calls=%fused_computation.95 | convolution fusion | flops 10884022272 | bytes 91423232 | tf_op jit(solution)/shard_map/dot_general | solution.py:147
  1079.1 198.4 %all-gather.26.cloned.1.call-done = bf16[9216,2304]{1,0:T(8,128)(2,1)} async-done(((bf16[288,2304]{1,0:T(8,128)(2,1)}), bf16[9216,2304]{1,0:T(8,128)(2,1)}) %all-gather.26.cloned.1.call-update) | async-done | bytes 42467344 | tf_op jit(solution)/shard_map/all_gather | solution.py:154
  1277.5 22.1 fusion.124
  1299.7 216.1 %all-gather.28.cloned.1.call-done = bf16[9216,2304]{1,0:T(8,128)(2,1)} async-done(((bf16[288,2304]{1,0:T(8,128)(2,1)}), bf16[9216,2304]{1,0:T(8,128)(2,1)}) %all-gather.28.cloned.1.call-update) | async-done | bytes 42467344 | tf_op jit(solution)/shard_map/all_gather | solution.py:153
  1515.8 34.2 %fusion.42 = f32[128,2304]{1,0:T(8,128)} fusion(bf16[9216,2304]{1,0:T(8,128)(2,1)} %all-gather.22.cloned.1.call-done, f32[128,9216]{1,0:T(8,128)} %fusion.123, f32[128,9216]{1,0:T(8,128)} %fusion.124, bf16[128,2304]{1,0:T(8,128)(2,1)} %copy-done.9, bf16[9216,2304]{1,0:T(8,128)(2,1)} %all-gather.28.cloned.1.call-done), kind=kOutput, calls=%fused_computation.60 | convolution fusion | flops 10896408576 | bytes 96141312 | tf_op jit(solution)/shard_map/dot_general | solution.py:161
  1550.0 22.0 multiply_reduce_fusion
  1576.5 6.9 convolution_convert_fusion
  1603.1 46.7 %reduce-scatter.16.cloned.1.call-done = bf16[128,2048]{1,0:T(8,128)(2,1)} async-done(((bf16[1024,2048]{1,0:T(8,128)(2,1)}), bf16[128,2048]{1,0:T(8,128)(2,1)}) %reduce-scatter.16.cloned.1.call-update) | async-done | bytes 524304
  1665.2 8.2 fusion.67
  1673.5 7.7 fusion.126
  1681.3 94.6 %all-gather.32.cloned.1.call-done = bf16[4096,2304]{1,0:T(8,128)(2,1)} async-done(((bf16[128,2304]{1,0:T(8,128)(2,1)}), bf16[4096,2304]{1,0:T(8,128)(2,1)}) %all-gather.32.cloned.1.call-update) | async-done | bytes 18874384 | tf_op jit(solution)/shard_map/all_gather | solution.py:164
  1775.9 11.5 fusion.129
  1787.4 12.9 fusion.128
  1807.7 42.2 %all-reduce.8 = (f32[2304]{0:T(1024)}, f32[2304]{0:T(1024)}, f32[2304]{0:T(1024)}, f32[2304]{0:T(1024)}) all-reduce(f32[2304]{0:T(1024)} %get-tuple-element.19, f32[2304]{0:T(1024)} %get-tuple-element.17, f32[2304]{0:T(1024)} %get-tuple-element.15, f32[2304]{0:T(1024)} %get-tuple-element.13), channel_id=7, replica_groups=mesh['batch'=4,'ctx'=8] {'batch','ctx'}, use_global_device_ids=true, to_apply=%region_18.19.clone | all-reduce | flops 9216 | bytes 73728
  1857.1 45.8 %all-gather.30.cloned.1.call-done = bf16[4096,2304]{1,0:T(8,128)(2,1)} async-done(((bf16[128,2304]{1,0:T(8,128)(2,1)}), bf16[4096,2304]{1,0:T(8,128)(2,1)}) %all-gather.30.cloned.1.call-update) | async-done | bytes 18874384 | tf_op jit(solution)/shard_map/all_gather | solution.py:165
  1902.8 13.2 fusion.127
  1916.1 16.9 fusion.32
  1933.0 11.2 fusion.33
  1944.3 21.0 fusion.34
  1965.3 78.5 %reduce-scatter.10.cloned.1.call-done = f32[72,1024]{1,0:T(8,128)} async-done(((f32[2304,1024]{1,0:T(8,128)}), f32[72,1024]{1,0:T(8,128)}) %reduce-scatter.10.cloned.1.call-update) | async-done | bytes 294928 | tf_op jit(solution)/shard_map/reduce_scatter | solution.py:225
  2043.7 141.5 %reduce-scatter.12.cloned.1.call-done = f32[72,1024]{1,0:T(8,128)} async-done(((f32[2304,1024]{1,0:T(8,128)}), f32[72,1024]{1,0:T(8,128)}) %reduce-scatter.12.cloned.1.call-update) | async-done | bytes 294928 | tf_op jit(solution)/shard_map/reduce_scatter | solution.py:226
  2185.2 212.6 %reduce-scatter.8.cloned.1.call-done = f32[72,2048]{1,0:T(8,128)} async-done(((f32[2304,2048]{1,0:T(8,128)}), f32[72,2048]{1,0:T(8,128)}) %reduce-scatter.8.cloned.1.call-update) | async-done | bytes 589840 | tf_op jit(solution)/shard_map/reduce_scatter | solution.py:224
  2397.9 212.8 %reduce-scatter.14.cloned.1.call-done = f32[64,2304]{1,0:T(8,128)} async-done(((f32[2048,2304]{1,0:T(8,128)}), f32[64,2304]{1,0:T(8,128)}) %reduce-scatter.14.cloned.1.call-update) | async-done | bytes 589840 | tf_op jit(solution)/shard_map/reduce_scatter | solution.py:227
  (195 shorter events, 113.9 us)
Async XLA Ops:
  7.2 70.2 %all-gather.14.cloned.1.call-start = ((), (), s32[]{:S(2)}) async-start(), calls=%async_computation.6 | async-start | bytes 4866048 | tf_op jit(solution)/shard_map/all_gather | solution.py:96
  7.9 134.4 %all-gather.12.cloned.1.call-start = ((), (), s32[]{:S(2)}) async-start(), calls=%async_computation.5 | async-start | bytes 4866048 | tf_op jit(solution)/shard_map/all_gather | solution.py:95
  8.7 183.0 %all-gather.16.cloned.1.call-start = ((), (), s32[]{:S(2)}) async-start(), calls=%async_computation.7 | async-start | bytes 4718592 | tf_op jit(solution)/shard_map/all_gather | solution.py:115
  58.2 216.7 %copy-start.2 = (bf16[128,2304]{1,0:T(8,128)(2,1)}, bf16[128,2304]{1,0:T(8,128)(2,1)S(1)}, u32[]{:S(2)}) copy-start(bf16[128,2304]{1,0:T(8,128)(2,1)S(1)} %multiply_convert_fusion.10) | copy-start | bytes 1769476
  80.5 67.6 %copy-start.10 = (bf16[288,2304]{1,0:T(8,128)(2,1)S(1)}, bf16[288,2304]{1,0:T(8,128)(2,1)}, u32[]{:S(2)}) copy-start(bf16[288,2304]{1,0:T(8,128)(2,1)} %param.26) | copy-start | bytes 3981316
  80.5 67.6 %copy-start.12 = (bf16[288,2304]{1,0:T(8,128)(2,1)S(1)}, bf16[288,2304]{1,0:T(8,128)(2,1)}, u32[]{:S(2)}) copy-start(bf16[288,2304]{1,0:T(8,128)(2,1)} %param.27) | copy-start | bytes 3981316
  146.3 128.6 %all-gather.18.cloned.1.call-start = ((), (), s32[]{:S(2)}) async-start(), calls=%async_computation.8 | async-start | bytes 9732096 | tf_op jit(solution)/shard_map/all_gather | solution.py:94
  146.9 211.0 %all-gather.20.cloned.1.call-start = ((), (), s32[]{:S(2)}) async-start(), calls=%async_computation.9 | async-start | bytes 9732096 | tf_op jit(solution)/shard_map/all_gather | solution.py:97
  147.5 448.9 %all-gather.22.cloned.1.call-start = ((), (), s32[]{:S(2)}) async-start(), calls=%async_computation.10 | async-start | bytes 43794432 | tf_op jit(solution)/shard_map/all_gather | solution.py:142
  148.1 891.2 %all-gather.24.cloned.1.call-start = ((), (), s32[]{:S(2)}) async-start(), calls=%async_computation.11 | async-start | bytes 87588864 | tf_op jit(solution)/shard_map/all_gather | solution.py:16
  149.9 1127.7 %all-gather.26.cloned.1.call-start = ((), (), s32[]{:S(2)}) async-start(), calls=%async_computation.12 | async-start | bytes 43794432 | tf_op jit(solution)/shard_map/all_gather | solution.py:154
  150.6 1365.2 %all-gather.28.cloned.1.call-start = ((), (), s32[]{:S(2)}) async-start(), calls=%async_computation.13 | async-start | bytes 43794432 | tf_op jit(solution)/shard_map/all_gather | solution.py:153
  151.4 1498.4 %reduce-scatter.16.cloned.1.call-start = ((), (), s32[]{:S(2)}) async-start(), calls=%async_computation.20 | async-start | bytes 4718592
  151.6 211.6 %copy-start.23 = (f32[2304]{0:T(1024)}, f32[2304]{0:T(1024)S(1)}, u32[]{:S(2)}) copy-start(f32[2304]{0:T(1024)S(1)} %convert_element_type.98) | copy-start | bytes 27652
  153.8 128.1 %copy-start.25 = (pred[128,1024]{0,1:T(8,128)(4,1)}, pred[128,1024]{0,1:T(8,128)(4,1)S(1)}, u32[]{:S(2)}) copy-start(pred[128,1024]{0,1:T(8,128)(4,1)S(1)} %broadcast_compare_fusion) | copy-start | bytes 393220
  207.2 73.1 %copy-start.16 = (bf16[1024,4,256,1]{0,2,3,1:T(8,128)(2,1)S(1)}, bf16[1024,4,256,1]{0,2,3,1:T(8,128)(2,1)}, u32[]{:S(2)}) copy-start(bf16[1024,4,256,1]{0,2,3,1:T(8,128)(2,1)} %copy.68) | copy-start | bytes 6291460
  285.6 77.6 %copy-start.7 = (bf16[128,4,2,256]{0,3,2,1:T(8,128)(2,1)}, bf16[128,4,2,256]{0,3,2,1:T(8,128)(2,1)S(1)}, u32[]{:S(2)}) copy-start(bf16[128,4,2,256]{0,3,2,1:T(8,128)(2,1)S(1)} %divide_convert_fusion) | copy-start | bytes 1572868
  363.6 232.7 %copy-start.29 = (f32[128]{0:T(128)}, f32[128]{0:T(128)S(1)}, u32[]{:S(2)}) copy-start(f32[128]{0:T(128)S(1)} %add_rsqrt_fusion.1) | copy-start | bytes 1540
  363.8 232.6 %copy-start.9 = (bf16[128,2304]{1,0:T(8,128)(2,1)}, bf16[128,2304]{1,0:T(8,128)(2,1)S(1)}, u32[]{:S(2)}) copy-start(bf16[128,2304]{1,0:T(8,128)(2,1)S(1)} %multiply_convert_fusion.9) | copy-start | bytes 1769476
  620.0 454.0 %copy-start.4 = (f32[1,128,2304]{2,1,0:T(8,128)S(1)}, f32[1,128,2304]{2,1,0:T(8,128)}, u32[]{:S(2)}) copy-start(f32[1,128,2304]{2,1,0:T(8,128)} %param.16) | copy-start | bytes 3538948
  1601.5 48.3 %copy-start.3 = (bf16[128,2304]{1,0:T(8,128)(2,1)S(1)}, bf16[128,2304]{1,0:T(8,128)(2,1)}, u32[]{:S(2)}) copy-start(bf16[128,2304]{1,0:T(8,128)(2,1)} %copy-done.2) | copy-start | bytes 1769476
  1601.6 174.3 %all-gather.32.cloned.1.call-start = ((), (), s32[]{:S(2)}) async-start(), calls=%async_computation.19 | async-start | bytes 19464192 | tf_op jit(solution)/shard_map/all_gather | solution.py:164
  1602.3 300.5 %all-gather.30.cloned.1.call-start = ((), (), s32[]{:S(2)}) async-start(), calls=%async_computation.18 | async-start | bytes 19464192 | tf_op jit(solution)/shard_map/all_gather | solution.py:165
  1602.9 440.9 %reduce-scatter.10.cloned.1.call-start = ((), (), s32[]{:S(2)}) async-start(), calls=%async_computation.15 | async-start | bytes 9732096 | tf_op jit(solution)/shard_map/reduce_scatter | solution.py:225
  1655.9 529.4 %reduce-scatter.12.cloned.1.call-start = ((), (), s32[]{:S(2)}) async-start(), calls=%async_computation.16 | async-start | bytes 9732096 | tf_op jit(solution)/shard_map/reduce_scatter | solution.py:226
  1662.1 735.8 %reduce-scatter.8.cloned.1.call-start = ((), (), s32[]{:S(2)}) async-start(), calls=%async_computation.14 | async-start | bytes 19464192 | tf_op jit(solution)/shard_map/reduce_scatter | solution.py:224
  1673.5 937.3 %reduce-scatter.14.cloned.1.call-start = ((), (), s32[]{:S(2)}) async-start(), calls=%async_computation.17 | async-start | bytes 19464192 | tf_op jit(solution)/shard_map/reduce_scatter | solution.py:227
  1681.3 106.1 %copy-start.11 = (bf16[288,2304]{1,0:T(8,128)(2,1)S(1)}, bf16[288,2304]{1,0:T(8,128)(2,1)}, u32[]{:S(2)}) copy-start(bf16[288,2304]{1,0:T(8,128)(2,1)} %param.26) | copy-start | bytes 3981316
  1805.2 50.5 %copy-start.6 = (f32[128,2304]{1,0:T(8,128)S(1)}, f32[128,2304]{1,0:T(8,128)}, u32[]{:S(2)}) copy-start(f32[128,2304]{1,0:T(8,128)} %copy-done.5) | copy-start | bytes 3538948
  1902.8 30.1 %slice-start.7 = ((s8[18874368]{0:T(1024)(128)(4,1)}), s8[4194304]{0:T(1024)(128)(4,1)S(1)}, s32[]{:S(2)}) async-start(s8[18874368]{0:T(1024)(128)(4,1)} %bitcast.162), calls=%async_computation.28 | async-start | bytes 8388608
  1902.8 30.1 %slice-start.8 = ((s8[18874368]{0:T(1024)(128)(4,1)}), s8[4194304]{0:T(1024)(128)(4,1)S(1)}, s32[]{:S(2)}) async-start(s8[18874368]{0:T(1024)(128)(4,1)} %bitcast.162), calls=%async_computation.29 | async-start | bytes 8388608
  1902.8 30.1 %slice-start.9 = ((s8[18874368]{0:T(1024)(128)(4,1)}), s8[4194304]{0:T(1024)(128)(4,1)S(1)}, s32[]{:S(2)}) async-start(s8[18874368]{0:T(1024)(128)(4,1)} %bitcast.162), calls=%async_computation.30 | async-start | bytes 8388608
  (31 other events, 262.5 us)
Sparse Core Ops, SparseCore 0:
  11.0 66.3 all-gather.13
  80.4 61.9 all-gather.11
  146.5 45.1 all-gather.15
  194.5 80.3 all-gather.17
  277.8 80.0 all-gather.19
  360.8 235.5 all-gather.21
  600.0 439.2 all-gather.23
  1042.3 235.1 all-gather.25
  1280.6 235.1 all-gather.27
  1601.7 48.0 reduce-scatter.15
  1653.4 122.4 all-gather.31
  1778.8 123.9 all-gather.29
  1909.3 134.4 reduce-scatter.9
  2050.1 135.1 reduce-scatter.11
  2192.1 205.7 reduce-scatter.7
  2404.7 205.9 reduce-scatter.13
